TPU v7x, 32 devices: a whole 2x2x4 slice. The times are simulated.
32 devices in a mesh: dp: 8 (over z, y), expert: 4 (over x, core).
Axes of the slice: x: 2, y: 2, z: 4, core: 2. Of those that a mesh axis runs over, the one named last changes fastest.
Arguments:
- tokens: bfloat16 [4096, 2048], P(('dp', 'expert')), may hold values from -6 to 6
- routes: int32 [4096, 8], P(('dp', 'expert')), may hold values from 0 to 15, all different within a row; in each aligned block of 128 rows (0 to 127, 128 to 255, ...) at most 80 rows name the same one
- gates: bfloat16 [4096, 8], P(('dp', 'expert')), may hold values from 0.099609375 to 0.5
- cotangent: bfloat16 [4096, 2048], P(('dp', 'expert')), may hold values from -6 to 6
- w_gate: bfloat16 [16, 2048, 384], P('dp'), may hold values from -0.125 to 0.125
- w_up: bfloat16 [16, 2048, 384], P('dp'), may hold values from -0.125 to 0.125
- w_down: bfloat16 [16, 384, 2048], P('dp'), may hold values from -0.3125 to 0.3125
Outputs:
- layer_out: bfloat16 [4096, 2048], P(('dp', 'expert'))
- grad_tokens: bfloat16 [4096, 2048], P(('dp', 'expert'))
- grad_gate: bfloat16 [16, 2048, 384], P('dp', 'expert')
- grad_up: bfloat16 [16, 2048, 384], P('dp', 'expert')
- grad_down: bfloat16 [16, 384, 2048], P('dp', None, 'expert')
Inputs may be any that keep to these rules, and one draw needn't show every extreme that they name: `routes`: each row names 8 different experts. Among the rows of one device, no expert is named by more than 80 rows, and in every draw some device has an expert named by exactly 80 rows.
All inputs are finite; a program needn't handle non-finite values.
Results may differ from a plain program's by a relative error of at most 0.012.
Values may be sent and summed in bfloat16 or wider, within the bound.
A program may use at most 128 MiB of HBM per device.

v0:
```python
import jax
import jax.numpy as jnp
from jax import lax
from jax.sharding import PartitionSpec as P


def expert_forward(arrived, w_gate, w_up, w_down):
    gate_act = jnp.einsum("erd,edf->erf", arrived, w_gate, preferred_element_type=jnp.float32)
    up_act = jnp.einsum("erd,edf->erf", arrived, w_up, preferred_element_type=jnp.float32)
    sigma_gate = jax.nn.sigmoid(gate_act)
    smooth = gate_act * sigma_gate
    hidden = (smooth * up_act).astype(jnp.bfloat16)
    result = jnp.einsum("erf,efd->erd", hidden, w_down, preferred_element_type=jnp.float32).astype(
        jnp.bfloat16
    )
    return (gate_act, up_act, sigma_gate, smooth, hidden, result)


def body(tokens, routes, gates, cotangent, w_gate, w_up, w_down):
    tok_rows, top_k = routes.shape
    width = tokens.shape[1]
    owners = lax.axis_size("dp")
    per_owner = w_gate.shape[0]
    hidden_units = w_gate.shape[2]
    experts = owners * per_owner
    capacity = max(2, tok_rows * top_k * 5 // (4 * experts))
    slot_count = experts * capacity
    chosen = routes.reshape(-1)
    onehot = (chosen[:, None] == jnp.arange(experts, dtype=jnp.int32)[None, :]).astype(jnp.int32)
    order_in = jnp.sum((jnp.cumsum(onehot, axis=0) - onehot) * onehot, axis=1)
    slot_index = chosen * capacity + order_in
    token_of = jnp.arange(tok_rows * top_k, dtype=jnp.int32) // top_k
    table = jnp.full((slot_count,), tok_rows, jnp.int32).at[slot_index].set(token_of)
    slot_gain = (
        jnp.zeros((slot_count,), jnp.float32)
        .at[slot_index]
        .set(gates.reshape(-1).astype(jnp.float32))
    )
    padded_x = jnp.concatenate([tokens, jnp.zeros((1, width), tokens.dtype)], axis=0)
    padded_c = jnp.concatenate([cotangent, jnp.zeros((1, width), cotangent.dtype)], axis=0)
    send_rows = padded_x[table].reshape(experts, capacity, width)
    send_grads = (slot_gain[:, None] * padded_c[table].astype(jnp.float32)).astype(jnp.bfloat16)
    send_grads = send_grads.reshape(experts, capacity, width)
    arrived = lax.all_to_all(send_rows, "dp", split_axis=0, concat_axis=1, tiled=True)
    state = expert_forward(arrived, w_gate, w_up, w_down)
    arrived_grad = lax.all_to_all(send_grads, "dp", split_axis=0, concat_axis=1, tiled=True)
    gate_act, up_act, sigma_gate, smooth, hidden, result = state
    returned = lax.all_to_all(result, "dp", split_axis=1, concat_axis=0, tiled=True).reshape(
        slot_count, width
    )
    picked = returned[slot_index].reshape(tok_rows, top_k, width)
    layer_out = jnp.einsum("tk,tkd->td", gates, picked, preferred_element_type=jnp.float32).astype(
        jnp.bfloat16
    )
    grad_hidden = jnp.einsum(
        "erd,efd->erf", arrived_grad, w_down, preferred_element_type=jnp.float32
    )
    grad_upact = (grad_hidden * smooth).astype(jnp.bfloat16)
    grad_gateact = (
        grad_hidden * up_act * sigma_gate * (1.0 + gate_act * (1.0 - sigma_gate))
    ).astype(jnp.bfloat16)
    row_grads = (
        jnp.einsum("erf,edf->erd", grad_gateact, w_gate, preferred_element_type=jnp.float32)
        + jnp.einsum("erf,edf->erd", grad_upact, w_up, preferred_element_type=jnp.float32)
    ).astype(jnp.bfloat16)
    came_back = lax.all_to_all(row_grads, "dp", split_axis=1, concat_axis=0, tiled=True).reshape(
        slot_count, width
    )
    grad_picked = came_back[slot_index].reshape(tok_rows, top_k, width)
    grad_tokens = jnp.sum(grad_picked.astype(jnp.float32), axis=1).astype(jnp.bfloat16)
    both_factors = jnp.concatenate([grad_gateact, grad_upact], axis=2)
    input_term = jnp.einsum(
        "erd,erf->def", arrived, both_factors, preferred_element_type=jnp.float32
    )
    down_term = jnp.einsum("erf,erd->def", hidden, arrived_grad, preferred_element_type=jnp.float32)
    totals = lax.psum_scatter(
        jnp.concatenate([input_term, down_term], axis=2).astype(jnp.bfloat16),
        "expert",
        scatter_dimension=0,
        tiled=True,
    ).astype(jnp.float32)
    grad_gate = jnp.transpose(totals[:, :, :hidden_units], (1, 0, 2)).astype(jnp.bfloat16)
    grad_up = jnp.transpose(totals[:, :, hidden_units : 2 * hidden_units], (1, 0, 2)).astype(
        jnp.bfloat16
    )
    grad_down = jnp.transpose(totals[:, :, 2 * hidden_units :], (1, 2, 0)).astype(jnp.bfloat16)
    return (layer_out, grad_tokens, grad_gate, grad_up, grad_down)


def solution(mesh):
    return jax.shard_map(
        body,
        mesh=mesh,
        in_specs=(
            P(("dp", "expert"), None),
            P(("dp", "expert"), None),
            P(("dp", "expert"), None),
            P(("dp", "expert"), None),
            P("dp", None, None),
            P("dp", None, None),
            P("dp", None, None),
        ),
        out_specs=(
            P(("dp", "expert"), None),
            P(("dp", "expert"), None),
            P("dp", "expert", None),
            P("dp", "expert", None),
            P("dp", None, "expert"),
        ),
        check_vma=False,
    )
```

profile of v0, /device:TPU:0, one launch (start us, length us, event | category | flops | bytes accessed | tf_op | source)
XLA Modules:
  0.0 628.1 jit_solution(449941669003016595)
XLA Ops:
  9.0 4.5 reduce-window.6
  25.7 11.9 %gather_fusion.2 = bf16[1280,2048]{1,0:T(8,128)(2,1)} fusion(bf16[129,2048]{1,0:T(8,128)(2,1)} %concatenate.14, s32[2048]{0:T(1024)S(1)} %pad_clamp_fusion), kind=kCustom, calls=%fused_computation.2 | custom fusion | bytes 10490880 | tf_op jit(solution)/shard_map/gather | solution.py:42
  37.7 5.7 fusion
  43.4 7.3 %all-to-all-start.2 = ((bf16[16,80,2048]{2,1,0:T(8,128)(2,1)}), bf16[16,80,2048]{2,1,0:T(8,128)(2,1)}, u32[]{:S(2)}, u32[]{:S(2)}) async-start(bf16[16,80,2048]{2,1,0:T(8,128)(2,1)} %fusion), calls=%async_computation.2 | async-start | bytes 10485760 | tf_op jit(solution)/shard_map/all_to_all | solution.py:46
  52.6 12.0 %gather_fusion = bf16[1280,2048]{1,0:T(8,128)(2,1)} fusion(bf16[129,2048]{1,0:T(8,128)(2,1)} %concatenate.13, s32[2048]{0:T(1024)S(1)} %pad_clamp_fusion), kind=kCustom, calls=%fused_computation | custom fusion | bytes 10490880 | tf_op jit(solution)/shard_map/gather | solution.py:41
  64.5 101.9 %all-to-all-done.2 = bf16[16,80,2048]{2,1,0:T(8,128)(2,1)} async-done(((bf16[16,80,2048]{2,1,0:T(8,128)(2,1)}), bf16[16,80,2048]{2,1,0:T(8,128)(2,1)}, u32[]{:S(2)}, u32[]{:S(2)}) %all-to-all-start.2) | async-done | bytes 5242912 | tf_op jit(solution)/shard_map/all_to_all | solution.py:46
  166.4 5.2 all-to-all-start
  171.6 5.6 copy.52
  177.3 109.3 %all-to-all-done = bf16[16,80,2048]{2,1,0:T(8,128)(2,1)} async-done(((bf16[16,80,2048]{2,1,0:T(8,128)(2,1)}), bf16[16,80,2048]{2,1,0:T(8,128)(2,1)}, u32[]{:S(2)}, u32[]{:S(2)}) %all-to-all-start) | async-done | bytes 5242912 | tf_op jit(solution)/shard_map/all_to_all | solution.py:44
  298.3 6.0 multiply_convert_fusion
  307.4 7.1 %convert_bitcast_fusion = bf16[2048,2,768]{0,2,1:T(8,128)(2,1)} fusion(bf16[2,640,2048]{2,1,0:T(8,128)(2,1)S(1)} %bitcast.86, bf16[2,640,384]{1,2,0:T(8,128)(2,1)S(1)} %copy-done.7, bf16[2,640,384]{1,2,0:T(8,128)(2,1)S(1)} %get-tuple-element.21), kind=kOutput, calls=%fused_computation.10 | convolution fusion | flops 4033609728 | bytes 13500416 | tf_op jit(solution)/shard_map/erd,erf->def/dot_general | solution.py:72
  318.6 5.2 add_convert_fusion
  323.7 10.2 %copy.55 = bf16[2,640,2048]{2,0,1:T(2,128)(2,1)} copy(bf16[2,640,2048]{2,1,0:T(8,128)(2,1)} %add_convert_fusion) | data formatting | bytes 10485760 | tf_op jit(solution)/shard_map/convert_element_type | solution.py:65
  334.0 4.7 all-to-all-start.3
  338.7 8.0 %pad_maximum_fusion = bf16[2048,2,1152]{0,2,1:T(8,128)(2,1)} fusion(bf16[2048,2,384]{0,2,1:T(8,128)(2,1)} %fusion.3, bf16[2048,2,768]{0,2,1:T(8,128)(2,1)} %convert_bitcast_fusion), kind=kLoop, calls=%fused_computation.9 | loop fusion | flops 18874368 | bytes 18874368 | tf_op jit(solution)/shard_map/concatenate | solution.py:77
  346.8 5.9 convolution_convert_fusion
  352.7 11.0 %copy.49 = bf16[2,640,2048]{2,0,1:T(2,128)(2,1)} copy(bf16[2,640,2048]{2,1,0:T(8,128)(2,1)} %convolution_convert_fusion) | data formatting | bytes 10485760 | tf_op jit(solution)/shard_map/convert_element_type | solution.py:13
  363.7 89.8 %all-to-all-done.3 = bf16[2,640,2048]{2,0,1:T(2,128)(2,1)} async-done(((bf16[2,640,2048]{2,0,1:T(2,128)(2,1)}), bf16[2,640,2048]{2,0,1:T(2,128)(2,1)}, u32[]{:S(2)}, u32[]{:S(2)}) %all-to-all-start.3) | async-done | bytes 5242912 | tf_op jit(solution)/shard_map/all_to_all | solution.py:66
  453.5 4.9 all-to-all-start.1
  458.6 7.2 %copy.56 = bf16[2,8,80,2048]{3,2,0,1:T(8,128)(2,1)} copy(bf16[2,8,80,2048]{3,0,2,1:T(2,128)(2,1)} %bitcast.18) | data formatting | bytes 10485760 | tf_op jit(solution)/shard_map/all_to_all | solution.py:66
  465.8 107.5 %all-to-all-done.1 = bf16[2,640,2048]{2,0,1:T(2,128)(2,1)} async-done(((bf16[2,640,2048]{2,0,1:T(2,128)(2,1)}), bf16[2,640,2048]{2,0,1:T(2,128)(2,1)}, u32[]{:S(2)}, u32[]{:S(2)}) %all-to-all-start.1) | async-done | bytes 5242912 | tf_op jit(solution)/shard_map/all_to_all | solution.py:48
  573.3 7.3 %copy.50 = bf16[2,8,80,2048]{3,2,0,1:T(8,128)(2,1)} copy(bf16[2,8,80,2048]{3,0,2,1:T(2,128)(2,1)} %bitcast.8) | data formatting | bytes 10485760 | tf_op jit(solution)/shard_map/all_to_all | solution.py:48
  580.6 12.0 %gather_fusion.3 = bf16[1024,2048]{1,0:T(8,128)(2,1)} fusion(bf16[1280,2048]{1,0:T(8,128)(2,1)} %bitcast.74, s32[1024]{0:T(1024)S(1)} %broadcast_clamp_fusion), kind=kCustom, calls=%fused_computation.3 | custom fusion | bytes 8392704 | tf_op jit(solution)/shard_map/gather | solution.py:69
  592.5 12.2 %gather_fusion.1 = bf16[1024,2048]{1,0:T(8,128)(2,1)} fusion(bf16[1280,2048]{1,0:T(8,128)(2,1)} %bitcast.75, s32[1024]{0:T(1024)S(1)} %broadcast_clamp_fusion), kind=kCustom, calls=%fused_computation.1 | custom fusion | bytes 8392704 | tf_op jit(solution)/shard_map/gather | solution.py:51
  (73 shorter events, 50.9 us)
Async XLA Ops:
  7.2 291.1 %copy-start = (bf16[2,384,2048]{2,1,0:T(8,128)(2,1)S(1)}, bf16[2,384,2048]{2,1,0:T(8,128)(2,1)}, u32[]{:S(2)}) copy-start(bf16[2,384,2048]{2,1,0:T(8,128)(2,1)} %param.13) | copy-start | bytes 9437188
  43.4 123.1 %all-to-all-start.2 = ((bf16[16,80,2048]{2,1,0:T(8,128)(2,1)}), bf16[16,80,2048]{2,1,0:T(8,128)(2,1)}, u32[]{:S(2)}, u32[]{:S(2)}) async-start(bf16[16,80,2048]{2,1,0:T(8,128)(2,1)} %fusion), calls=%async_computation.2 | async-start | bytes 10485760 | tf_op jit(solution)/shard_map/all_to_all | solution.py:46
  166.4 120.1 %all-to-all-start = ((bf16[16,80,2048]{2,1,0:T(8,128)(2,1)}), bf16[16,80,2048]{2,1,0:T(8,128)(2,1)}, u32[]{:S(2)}, u32[]{:S(2)}) async-start(bf16[16,80,2048]{2,1,0:T(8,128)(2,1)} %bitcast.76), calls=%async_computation | async-start | bytes 10485760 | tf_op jit(solution)/shard_map/all_to_all | solution.py:44
  286.5 3.4 copy-start.4
  289.6 4.5 copy-start.2
  290.0 4.2 copy-start.5
  290.0 8.3 %slice-start = ((s8[5242880]{0:T(1024)(128)(4,1)}), s8[4194304]{0:T(1024)(128)(4,1)S(1)}, s32[]{:S(2)}) async-start(s8[5242880]{0:T(1024)(128)(4,1)} %bitcast.78), calls=%async_computation.6 | async-start | bytes 8388608
  294.1 4.1 slice-start.1
  304.2 3.2 copy-start.3
  304.2 3.2 copy-start.7
  304.2 10.3 %slice-start.2 = ((s8[5242880]{0:T(1024)(128)(4,1)}), s8[4194304]{0:T(1024)(128)(4,1)S(1)}, s32[]{:S(2)}) async-start(s8[5242880]{0:T(1024)(128)(4,1)} %bitcast.81), calls=%async_computation.8 | async-start | bytes 8388608
  307.4 7.1 %slice-start.3 = ((s8[5242880]{0:T(1024)(128)(4,1)}), s8[1048576]{0:T(1024)(128)(4,1)S(1)}, s32[]{:S(2)}) async-start(s8[5242880]{0:T(1024)(128)(4,1)} %bitcast.81), calls=%async_computation.9 | async-start | bytes 2097152
  307.4 7.1 %copy-start.10 = (bf16[2,640,384]{1,2,0:T(8,128)(2,1)S(1)}, bf16[2,640,384]{1,2,0:T(8,128)(2,1)}, u32[]{:S(2)}) copy-start(bf16[2,640,384]{1,2,0:T(8,128)(2,1)} %get-tuple-element.22) | copy-start | bytes 2949124
  314.5 4.0 copy-start.6
  314.6 4.0 copy-start.8
  334.0 119.6 %all-to-all-start.3 = ((bf16[2,640,2048]{2,0,1:T(2,128)(2,1)}), bf16[2,640,2048]{2,0,1:T(2,128)(2,1)}, u32[]{:S(2)}, u32[]{:S(2)}) async-start(bf16[2,640,2048]{2,0,1:T(2,128)(2,1)} %copy.55), calls=%async_computation.3 | async-start | bytes 10485760 | tf_op jit(solution)/shard_map/all_to_all | solution.py:66
  338.7 274.5 %reduce-scatter.2.cloned.1.call-start = ((), (), s32[]{:S(2)}) async-start(), calls=%async_computation.5 | async-start | bytes 11796480 | tf_op jit(solution)/shard_map/reduce_scatter | solution.py:76
  363.7 94.7 %copy-start.9 = (bf16[128,8]{0,1:T(8,128)(2,1)S(1)}, bf16[128,8]{0,1:T(8,128)(2,1)}, u32[]{:S(2)}) copy-start(bf16[128,8]{0,1:T(8,128)(2,1)} %param.9) | copy-start | bytes 6148
  453.5 119.8 %all-to-all-start.1 = ((bf16[2,640,2048]{2,0,1:T(2,128)(2,1)}), bf16[2,640,2048]{2,0,1:T(2,128)(2,1)}, u32[]{:S(2)}, u32[]{:S(2)}) async-start(bf16[2,640,2048]{2,0,1:T(2,128)(2,1)} %copy.49), calls=%async_computation.1 | async-start | bytes 10485760 | tf_op jit(solution)/shard_map/all_to_all | solution.py:48
  604.8 4.7 copy-start.1
Sparse Core Ops, SparseCore 0:
  346.9 79.0 reduce-scatter.1
where the time goes:
time: 635 us; the launch traced here: 628 us
  waiting for transfers between devices  408 us (64%)
  local copies, waits for them, and re-layouts  117 us (18%)
  matrix products  43.1 us (7%)
  other arithmetic  22.8 us (4%)
  starting transfers between devices  22.1 us (3%)
  between operations  14.8 us (2%)
    all_to_all x1, waiting for transfers between devices, body(): lax.all_to_all(send_rows, 'dp', split_axis=0, concat_axis=1, tiled=True)  109 us
    all_to_all x1, waiting for transfers between devices, body(): lax.all_to_all(result, 'dp', split_axis=1, concat_axis=0, tiled=True)  107 us
    all_to_all x1, waiting for transfers between devices, body(): lax.all_to_all(send_grads, 'dp', split_axis=0, concat_axis=1, tiled=True)  102 us
    all_to_all x1, waiting for transfers between devices, body(): lax.all_to_all(row_grads, 'dp', split_axis=1, concat_axis=0, tiled=True)  89.8 us
  transfers between devices with their start and end apart: 5, of which 4 were waited for; matrix products, arithmetic and copies ran while one was open for 15% of the time, Pallas kernels for 0%

commit v1 on v0

--- a/solution.py
+++ b/solution.py
@@ -20,38 +20,38 @@
     tok_rows, top_k = routes.shape
     width = tokens.shape[1]
     owners = lax.axis_size("dp")
+    me = lax.axis_index("dp")
     per_owner = w_gate.shape[0]
     hidden_units = w_gate.shape[2]
     experts = owners * per_owner
     capacity = max(2, tok_rows * top_k * 5 // (4 * experts))
-    slot_count = experts * capacity
-    chosen = routes.reshape(-1)
-    onehot = (chosen[:, None] == jnp.arange(experts, dtype=jnp.int32)[None, :]).astype(jnp.int32)
-    order_in = jnp.sum((jnp.cumsum(onehot, axis=0) - onehot) * onehot, axis=1)
-    slot_index = chosen * capacity + order_in
-    token_of = jnp.arange(tok_rows * top_k, dtype=jnp.int32) // top_k
-    table = jnp.full((slot_count,), tok_rows, jnp.int32).at[slot_index].set(token_of)
-    slot_gain = (
-        jnp.zeros((slot_count,), jnp.float32)
-        .at[slot_index]
-        .set(gates.reshape(-1).astype(jnp.float32))
-    )
-    padded_x = jnp.concatenate([tokens, jnp.zeros((1, width), tokens.dtype)], axis=0)
-    padded_c = jnp.concatenate([cotangent, jnp.zeros((1, width), cotangent.dtype)], axis=0)
-    send_rows = padded_x[table].reshape(experts, capacity, width)
-    send_grads = (slot_gain[:, None] * padded_c[table].astype(jnp.float32)).astype(jnp.bfloat16)
-    send_grads = send_grads.reshape(experts, capacity, width)
-    arrived = lax.all_to_all(send_rows, "dp", split_axis=0, concat_axis=1, tiled=True)
-    state = expert_forward(arrived, w_gate, w_up, w_down)
-    arrived_grad = lax.all_to_all(send_grads, "dp", split_axis=0, concat_axis=1, tiled=True)
-    gate_act, up_act, sigma_gate, smooth, hidden, result = state
-    returned = lax.all_to_all(result, "dp", split_axis=1, concat_axis=0, tiled=True).reshape(
-        slot_count, width
-    )
-    picked = returned[slot_index].reshape(tok_rows, top_k, width)
-    layer_out = jnp.einsum("tk,tkd->td", gates, picked, preferred_element_type=jnp.float32).astype(
+    rows_per_expert = owners * capacity
+    both = jnp.concatenate([tokens, cotangent], axis=1)
+    all_both = lax.all_gather(both, "dp", axis=0, tiled=True)
+    all_routes = lax.all_gather(routes, "dp", axis=0, tiled=True)
+    all_gates = lax.all_gather(gates, "dp", axis=0, tiled=True)
+    all_x = all_both[:, :width]
+    all_c = all_both[:, width:]
+    mine = me * per_owner + jnp.arange(per_owner, dtype=jnp.int32)
+    hit = all_routes[None, :, :] == mine[:, None, None]
+    named = jnp.any(hit, axis=2).astype(jnp.int32)
+    gain = jnp.sum(jnp.where(hit, all_gates[None, :, :].astype(jnp.float32), 0.0), axis=2)
+    position = jnp.where(named > 0, jnp.cumsum(named, axis=1) - 1, -1)
+    pick = position[:, None, :] == jnp.arange(rows_per_expert, dtype=jnp.int32)[None, :, None]
+    pick_x = pick.astype(jnp.bfloat16)
+    pick_g = jnp.where(pick, gain[:, None, :], 0.0).astype(jnp.bfloat16)
+    arrived = jnp.einsum("ept,td->epd", pick_x, all_x, preferred_element_type=jnp.float32).astype(
         jnp.bfloat16
     )
+    arrived_grad = jnp.einsum(
+        "ept,td->epd", pick_g, all_c, preferred_element_type=jnp.float32
+    ).astype(jnp.bfloat16)
+    state = expert_forward(arrived, w_gate, w_up, w_down)
+    gate_act, up_act, sigma_gate, smooth, hidden, result = state
+    out_part = jnp.einsum("ept,epd->td", pick_g, result, preferred_element_type=jnp.float32).astype(
+        jnp.bfloat16
+    )
+    layer_out = lax.psum_scatter(out_part, "dp", scatter_dimension=0, tiled=True)
     grad_hidden = jnp.einsum(
         "erd,efd->erf", arrived_grad, w_down, preferred_element_type=jnp.float32
     )
@@ -63,11 +63,10 @@
         jnp.einsum("erf,edf->erd", grad_gateact, w_gate, preferred_element_type=jnp.float32)
         + jnp.einsum("erf,edf->erd", grad_upact, w_up, preferred_element_type=jnp.float32)
     ).astype(jnp.bfloat16)
-    came_back = lax.all_to_all(row_grads, "dp", split_axis=1, concat_axis=0, tiled=True).reshape(
-        slot_count, width
-    )
-    grad_picked = came_back[slot_index].reshape(tok_rows, top_k, width)
-    grad_tokens = jnp.sum(grad_picked.astype(jnp.float32), axis=1).astype(jnp.bfloat16)
+    grad_part = jnp.einsum(
+        "ept,epd->td", pick_x, row_grads, preferred_element_type=jnp.float32
+    ).astype(jnp.bfloat16)
+    grad_tokens = lax.psum_scatter(grad_part, "dp", scatter_dimension=0, tiled=True)
     both_factors = jnp.concatenate([grad_gateact, grad_upact], axis=2)
     input_term = jnp.einsum(
         "erd,erf->def", arrived, both_factors, preferred_element_type=jnp.float32

time: 635 us -> 452 us (0.71); the launches traced: 628 us -> 452 us
  waiting for transfers between devices: 408 us -> 281 us
  local copies, waits for them, and re-layouts: 117 us -> 7.89 us
  blocking collectives: 0 us -> 60.5 us
  matrix products: 43.1 us -> 75.8 us
  starting transfers between devices: 22.1 us -> 0.38 us
  other arithmetic: 22.8 us -> 12 us
    all_to_all x4 -> x0, waiting for transfers between devices: 408 us -> none  [the longest x1 109 us: body(): lax.all_to_all(send_rows, 'dp', split_axis=0, concat_axis=1, tiled=True)]
    reduce_scatter x0 -> x2, waiting for transfers between devices: none -> 177 us  [the longest x1 92 us: body(): lax.psum_scatter(grad_part, 'dp', scatter_dimension=0, tiled=True)]
    all_gather x0 -> x1, waiting for transfers between devices: none -> 66.1 us  [body(): all_both = lax.all_gather(both, 'dp', axis=0, tiled=True)]
    all_gather x0 -> x2, blocking collectives: none -> 60.5 us  [the longest x1 31.7 us: body(): all_routes = lax.all_gather(routes, 'dp', axis=0, tiled=True)]
    gather x4 -> x0, local copies, waits for them, and re-layouts: 48.1 us -> none  [the longest x1 12.2 us: body(): picked = returned[slot_index].reshape(tok_rows, top_k, width)]
    reduce_scatter x1, waiting for transfers between devices: 0.01 us -> 37.9 us  [body(): lax.psum_scatter(jnp.concatenate([input_term, down_term], axis=2).astype(...]
    dot_general x2 -> x4, matrix products: 8.74 us -> 40.2 us  [the longest x1 16.5 us: body(): jnp.einsum('ept,epd->td', pick_x, row_grads, preferred_element_type=jnp.f...]
    all_to_all x4 -> x0, local copies, waits for them, and re-layouts: 23.2 us -> none  [the longest x1 7.26 us: body(): lax.all_to_all(result, 'dp', split_axis=1, concat_axis=0, tiled=True)]
  transfers between devices with their start and end apart: 5 -> 4, of which waited for: 4 -> 4; matrix products, arithmetic and copies ran while one was open for 15% -> 10% of each run, Pallas kernels for 0% -> 0%
where the time goes in v1:
time: 452 us
  waiting for transfers between devices  281 us (62%)
  matrix products  75.8 us (17%)
  blocking collectives  60.5 us (13%)
  between operations  14 us (3%)
  other arithmetic  12 us (3%)
  local copies, waits for them, and re-layouts  7.89 us (2%)
    reduce_scatter x1, waiting for transfers between devices, body(): lax.psum_scatter(grad_part, 'dp', scatter_dimension=0, tiled=True)  92 us
    reduce_scatter x1, waiting for transfers between devices, body(): lax.psum_scatter(out_part, 'dp', scatter_dimension=0, tiled=True)  84.9 us
    all_gather x1, waiting for transfers between devices, body(): all_both = lax.all_gather(both, 'dp', axis=0, tiled=True)  66.1 us
    reduce_scatter x1, waiting for transfers between devices, body(): lax.psum_scatter(jnp.concatenate([input_term, down_term], axis=2).astype(...  37.9 us
    all_gather x1, blocking collectives, body(): all_routes = lax.all_gather(routes, 'dp', axis=0, tiled=True)  31.7 us
    all_gather x1, blocking collectives, body(): all_gates = lax.all_gather(gates, 'dp', axis=0, tiled=True)  28.8 us
    dot_general x1, matrix products, body(): jnp.einsum('ept,epd->td', pick_x, row_grads, preferred_element_type=jnp.f...  16.5 us
    dot_general x1, matrix products, body(): jnp.einsum('erf,edf->erd', grad_gateact, w_gate, preferred_element_type=j...  9.57 us
  transfers between devices with their start and end apart: 4, of which 4 were waited for; matrix products, arithmetic and copies ran while one was open for 10% of the time, Pallas kernels for 0%

profile of v1, /device:TPU:0, one launch (start us, length us, event | category | flops | bytes accessed | tf_op | source)
XLA Modules:
  0.0 451.6 jit_solution(4144293296469988950)
XLA Ops:
  7.2 2.5 pad_maximum_fusion.1
  9.8 28.8 %all_gather.10 = bf16[1024,8]{0,1:T(8,128)(2,1)S(1)} all-gather(bf16[128,8]{0,1:T(8,128)(2,1)} %param.9), channel_id=1, replica_groups=mesh['dp'=8,'expert'=4] {'dp'}, dimensions={0}, use_global_device_ids=true | all-gather | bytes 18432 | tf_op jit(solution)/shard_map/all_gather | solution.py:32
  38.6 31.7 %all_gather.9 = s32[1024,8]{0,1:T(8,128)S(1)} all-gather(s32[128,8]{0,1:T(8,128)} %param.8), channel_id=1, replica_groups=mesh['dp'=8,'expert'=4] {'dp'}, dimensions={0}, use_global_device_ids=true | all-gather | bytes 36864 | tf_op jit(solution)/shard_map/all_gather | solution.py:31
  70.4 0.6 reduce-window.6
  71.6 66.1 %all-gather.2.cloned.1.call-done = bf16[1024,4096]{1,0:T(8,128)(2,1)} async-done(((bf16[128,4096]{1,0:T(8,128)(2,1)}), bf16[1024,4096]{1,0:T(8,128)(2,1)}) %all-gather.2.cloned.1.call-update) | async-done | bytes 8388624 | tf_op jit(solution)/shard_map/all_gather | solution.py:30
  137.7 8.4 %fusion.6 = bf16[2,640,2048]{2,1,0:T(8,128)(2,1)S(1)} fusion(bf16[1024,4096]{1,0:T(8,128)(2,1)} %all-gather.2.cloned.1.call-done, s32[2,1024]{1,0:T(2,128)S(1)} %compare_select_fusion.1), kind=kOutput, calls=%fused_computation.15 | convolution fusion | flops 5372641280 | bytes 9445376 | tf_op jit(solution)/shard_map/ept,td->epd/dot_general | solution.py:43
  146.2 2.9 fusion.31
  149.1 4.1 fusion.30
  153.2 7.9 %fusion.5 = bf16[2,640,2048]{2,1,0:T(8,128)(2,1)} fusion(bf16[1024,4096]{1,0:T(8,128)(2,1)S(1)} %bitcast.63, bf16[2,1024]{1,0:T(2,128)(2,1)S(1)} %fusion.26, s32[2,1024]{1,0:T(2,128)S(1)} %compare_select_fusion.1), kind=kOutput, calls=%fused_computation.14 | convolution fusion | flops 5373952000 | bytes 9449472 | tf_op jit(solution)/shard_map/ept,td->epd/dot_general | solution.py:46
  161.1 6.5 %multiply_convert_fusion = (bf16[2,640,384]{1,2,0:T(8,128)(2,1)S(1)}, bf16[2,640,384]{1,2,0:T(8,128)(2,1)S(1)}, bf16[2,640,384]{1,2,0:T(8,128)(2,1)S(1)}) fusion(f32[2,640,384]{1,2,0:T(8,128)} %fusion.30, f32[2,640,384]{1,2,0:T(8,128)S(1)} %fusion.31, bf16[2,640,2048]{2,1,0:T(8,128)(2,1)} %fusion.5, bf16[2,384,2048]{2,1,0:T(8,128)(2,1)S(1)} %copy-done), kind=kOutput, calls=%fused_computation.30 | convolution fusion | flops 2020638720 | bytes 15269888 | tf_op jit(solution)/shard_map/erd,efd->erf/dot_general | solution.py:55
  167.7 2.9 fusion.9
  170.6 5.3 %convert_bitcast_fusion = bf16[2048,2,768]{0,2,1:T(8,128)(2,1)S(1)} fusion(bf16[2,640,2048]{2,1,0:T(8,128)(2,1)S(1)} %fusion.6, bf16[2,640,384]{1,2,0:T(8,128)(2,1)S(1)} %get-tuple-element.20, bf16[2,640,384]{1,2,0:T(8,128)(2,1)S(1)} %get-tuple-element.21), kind=kOutput, calls=%fused_computation.4 | convolution fusion | flops 4033609728 | bytes 13500416 | tf_op jit(solution)/shard_map/erd,erf->def/dot_general | solution.py:71
  175.9 8.5 %pad_maximum_fusion = bf16[2048,2,1152]{0,2,1:T(8,128)(2,1)} fusion(bf16[2048,2,384]{0,2,1:T(8,128)(2,1)S(1)} %fusion.9, bf16[2048,2,768]{0,2,1:T(8,128)(2,1)S(1)} %convert_bitcast_fusion), kind=kLoop, calls=%fused_computation.1 | loop fusion | flops 18874368 | bytes 18874368 | tf_op jit(solution)/shard_map/concatenate | solution.py:76
  184.4 4.4 fusion.59
  188.8 7.4 %bitcast_convert_fusion.1 = bf16[1024,2048]{1,0:T(8,128)(2,1)} fusion(bf16[2,1024]{1,0:T(2,128)(2,1)S(1)} %fusion.26, s32[2,1024]{1,0:T(2,128)S(1)} %compare_select_fusion.1, bf16[2,640,2048]{2,1,0:T(8,128)(2,1)S(1)} %fusion.59), kind=kOutput, calls=%fused_computation.3 | convolution fusion | flops 5373427712 | bytes 9449472 | tf_op jit(solution)/shard_map/ept,epd->td/dot_general | solution.py:51
  196.2 0.3 reduce-scatter.6.cloned.1.call-start
  196.5 9.6 %fusion.32 = f32[2,640,2048]{2,1,0:T(8,128)} fusion(bf16[2,640,384]{1,2,0:T(8,128)(2,1)} %copy-done.2, bf16[2,2048,384]{2,1,0:T(8,128)(2,1)} %param.11), kind=kOutput, calls=%fused_computation.54 | convolution fusion | flops 2013265920 | bytes 14614528 | tf_op jit(solution)/shard_map/erf,edf->erd/dot_general | solution.py:63
  206.1 16.5 %bitcast_convert_fusion = bf16[1024,2048]{1,0:T(8,128)(2,1)} fusion(f32[2,640,2048]{2,1,0:T(8,128)} %fusion.32, s32[2,1024]{1,0:T(2,128)S(1)} %compare_select_fusion.1, bf16[2,640,384]{1,2,0:T(8,128)(2,1)} %copy-done.6, bf16[2,2048,384]{2,1,0:T(8,128)(2,1)} %param.12), kind=kOutput, calls=%fused_computation.2 | convolution fusion | flops 7390625792 | bytes 18817024 | tf_op jit(solution)/shard_map/ept,epd->td/dot_general | solution.py:66
  222.6 37.9 %reduce-scatter.8.cloned.1.call-done = bf16[512,2,1152]{0,2,1:T(8,128)(2,1)} async-done(((bf16[2048,2,1152]{0,2,1:T(8,128)(2,1)}), bf16[512,2,1152]{0,2,1:T(8,128)(2,1)}) %reduce-scatter.8.cloned.1.call-update) | async-done | bytes 2359312 | tf_op jit(solution)/shard_map/reduce_scatter | solution.py:75
  260.5 3.1 slice_bitcast_fusion.8
  263.6 2.3 copy.36
  265.8 2.3 copy.35
  268.1 84.9 %reduce-scatter.4.cloned.1.call-done = bf16[128,2048]{1,0:T(8,128)(2,1)} async-done(((bf16[1024,2048]{1,0:T(8,128)(2,1)}), bf16[128,2048]{1,0:T(8,128)(2,1)}) %reduce-scatter.4.cloned.1.call-update) | async-done | bytes 524304 | tf_op jit(solution)/shard_map/reduce_scatter | solution.py:54
  353.1 92.0 %reduce-scatter.6.cloned.1.call-done = bf16[128,2048]{1,0:T(8,128)(2,1)} async-done(((bf16[1024,2048]{1,0:T(8,128)(2,1)}), bf16[128,2048]{1,0:T(8,128)(2,1)}) %reduce-scatter.6.cloned.1.call-update) | async-done | bytes 524304 | tf_op jit(solution)/shard_map/reduce_scatter | solution.py:69
  (36 shorter events, 0.9 us)
Async XLA Ops:
  7.2 154.0 %copy-start = (bf16[2,384,2048]{2,1,0:T(8,128)(2,1)S(1)}, bf16[2,384,2048]{2,1,0:T(8,128)(2,1)}, u32[]{:S(2)}) copy-start(bf16[2,384,2048]{2,1,0:T(8,128)(2,1)} %param.13) | copy-start | bytes 9437188
  7.2 130.6 %all-gather.2.cloned.1.call-start = ((), (), s32[]{:S(2)}) async-start(), calls=%async_computation.3 | async-start | bytes 9437184 | tf_op jit(solution)/shard_map/all_gather | solution.py:30
  9.7 250.8 %reduce-scatter.8.cloned.1.call-start = ((), (), s32[]{:S(2)}) async-start(), calls=%async_computation.6 | async-start | bytes 11796480 | tf_op jit(solution)/shard_map/reduce_scatter | solution.py:75
  137.7 8.4 %copy-start.3 = (bf16[2,2048,384]{2,1,0:T(8,128)(2,1)S(1)}, bf16[2,2048,384]{2,1,0:T(8,128)(2,1)}, u32[]{:S(2)}) copy-start(bf16[2,2048,384]{2,1,0:T(8,128)(2,1)} %param.12) | copy-start | bytes 9437188
  146.1 2.9 copy-start.1
  146.1 7.1 %slice-start = ((s8[8388608]{0:T(1024)(128)(4,1)}), s8[4194304]{0:T(1024)(128)(4,1)S(1)}, s32[]{:S(2)}) async-start(s8[8388608]{0:T(1024)(128)(4,1)} %bitcast.62), calls=%async_computation.7 | async-start | bytes 8388608
  149.1 4.2 slice-start.1
  161.1 6.5 %copy-start.5 = (bf16[2,640,2048]{2,1,0:T(8,128)(2,1)S(1)}, bf16[2,640,2048]{2,1,0:T(8,128)(2,1)}, u32[]{:S(2)}) copy-start(bf16[2,640,2048]{2,1,0:T(8,128)(2,1)} %fusion.5) | copy-start | bytes 15728644
  167.6 2.9 copy-start.4
  167.6 2.9 copy-start.2
  167.6 2.9 copy-start.6
  184.4 168.7 %reduce-scatter.4.cloned.1.call-start = ((), (), s32[]{:S(2)}) async-start(), calls=%async_computation.4 | async-start | bytes 4718592 | tf_op jit(solution)/shard_map/reduce_scatter | solution.py:54
  196.2 248.8 %reduce-scatter.6.cloned.1.call-start = ((), (), s32[]{:S(2)}) async-start(), calls=%async_computation.5 | async-start | bytes 4718592 | tf_op jit(solution)/shard_map/reduce_scatter | solution.py:69
Sparse Core Ops, SparseCore 0:
  10.1 127.5 all-gather.1
  184.5 75.9 reduce-scatter.7
  264.7 88.2 reduce-scatter.3
  357.1 87.9 reduce-scatter.5

commit v2 on v1

--- a/solution.py
+++ b/solution.py
@@ -26,12 +26,15 @@
     experts = owners * per_owner
     capacity = max(2, tok_rows * top_k * 5 // (4 * experts))
     rows_per_expert = owners * capacity
-    both = jnp.concatenate([tokens, cotangent], axis=1)
+    side = jnp.zeros((tok_rows, 128 - 2 * top_k), jnp.bfloat16)
+    both = jnp.concatenate(
+        [tokens, cotangent, routes.astype(jnp.bfloat16), gates.astype(jnp.bfloat16), side], axis=1
+    )
     all_both = lax.all_gather(both, "dp", axis=0, tiled=True)
-    all_routes = lax.all_gather(routes, "dp", axis=0, tiled=True)
-    all_gates = lax.all_gather(gates, "dp", axis=0, tiled=True)
     all_x = all_both[:, :width]
-    all_c = all_both[:, width:]
+    all_c = all_both[:, width : 2 * width]
+    all_routes = all_both[:, 2 * width : 2 * width + top_k].astype(jnp.int32)
+    all_gates = all_both[:, 2 * width + top_k : 2 * width + 2 * top_k]
     mine = me * per_owner + jnp.arange(per_owner, dtype=jnp.int32)
     hit = all_routes[None, :, :] == mine[:, None, None]
     named = jnp.any(hit, axis=2).astype(jnp.int32)
@@ -66,7 +69,11 @@
     grad_part = jnp.einsum(
         "ept,epd->td", pick_x, row_grads, preferred_element_type=jnp.float32
     ).astype(jnp.bfloat16)
-    grad_tokens = lax.psum_scatter(grad_part, "dp", scatter_dimension=0, tiled=True)
+    returned = lax.psum_scatter(
+        jnp.concatenate([out_part, grad_part], axis=1), "dp", scatter_dimension=0, tiled=True
+    )
+    layer_out = returned[:, :width]
+    grad_tokens = returned[:, width:]
     both_factors = jnp.concatenate([grad_gateact, grad_upact], axis=2)
     input_term = jnp.einsum(
         "erd,erf->def", arrived, both_factors, preferred_element_type=jnp.float32

time: 452 us -> 464 us (1.027)
  blocking collectives: 60.5 us -> 0 us
  waiting for transfers between devices: 281 us -> 331 us
  local copies, waits for them, and re-layouts: 7.89 us -> 21.9 us
  other arithmetic: 12 us -> 18.7 us
    all_gather x1, waiting for transfers between devices: 66.1 us -> 131 us  [body(): all_both = lax.all_gather(both, 'dp', axis=0, tiled=True)]
    all_gather x2 -> x0, blocking collectives: 60.5 us -> none  [the longest x1 31.7 us: body(): all_routes = lax.all_gather(routes, 'dp', axis=0, tiled=True)]
    reduce_scatter x2 -> x1, waiting for transfers between devices: 177 us -> 123 us  [body(): lax.psum_scatter(jnp.concatenate([out_part, grad_part], axis=1), 'dp', sc...]
    reduce_scatter x1, waiting for transfers between devices: 37.9 us -> 77.1 us  [body(): lax.psum_scatter(jnp.concatenate([input_term, down_term], axis=2).astype(...]
    unnamed x21 -> x32, local copies, waits for them, and re-layouts: 4.62 us -> 15.6 us
    concatenate x1, other arithmetic: 2.49 us -> 7.86 us  [body(): jnp.concatenate([out_part, grad_part], axis=1)]
  transfers between devices with their start and end apart: 4 -> 3, of which waited for: 4 -> 3; matrix products, arithmetic and copies ran while one was open for 10% -> 5% of each run, Pallas kernels for 0% -> 0%
where the time goes in v2:
time: 464 us; the launch traced here: 463 us
  waiting for transfers between devices  331 us (71%)
  matrix products  77.4 us (17%)
  local copies, waits for them, and re-layouts  21.9 us (5%)
  other arithmetic  18.7 us (4%)
  between operations  13.9 us (3%)
    all_gather x1, waiting for transfers between devices, body(): all_both = lax.all_gather(both, 'dp', axis=0, tiled=True)  131 us
    reduce_scatter x1, waiting for transfers between devices, body(): lax.psum_scatter(jnp.concatenate([out_part, grad_part], axis=1), 'dp', sc...  123 us
    reduce_scatter x1, waiting for transfers between devices, body(): lax.psum_scatter(jnp.concatenate([input_term, down_term], axis=2).astype(...  77.1 us
    unnamed x32, local copies, waits for them, and re-layouts  15.6 us
    dot_general x1, matrix products, body(): jnp.einsum('ept,epd->td', pick_x, row_grads, preferred_element_type=jnp.f...  15 us
  transfers between devices with their start and end apart: 3, of which 3 were waited for; matrix products, arithmetic and copies ran while one was open for 5% of the time, Pallas kernels for 0%

profile of v2, /device:TPU:0, one launch (start us, length us, event | category | flops | bytes accessed | tf_op | source)
XLA Modules:
  0.0 463.3 jit_solution(15104655544222967402)
XLA Ops:
  7.2 2.2 copy.41
  9.4 2.0 copy.42
  11.5 1.9 constant_dynamic-update-slice_fusion.3
  17.2 130.9 %all-gather.2.cloned.1.call-done = bf16[1024,4224]{0,1:T(8,128)(2,1)} async-done(((bf16[128,4224]{0,1:T(8,128)(2,1)}), bf16[1024,4224]{0,1:T(8,128)(2,1)}) %all-gather.2.cloned.1.call-update) | async-done | bytes 8650768 | tf_op jit(solution)/shard_map/all_gather | solution.py:33
  150.2 8.9 %fusion.7 = bf16[2,640,2048]{2,1,0:T(8,128)(2,1)S(1)} fusion(bf16[1024,4224]{0,1:T(8,128)(2,1)} %all-gather.2.cloned.1.call-done, bf16[2,1024]{1,0:T(2,128)(2,1)S(1)} %fusion.28, s32[2,1024]{1,0:T(2,128)S(1)} %compare_select_fusion.1), kind=kOutput, calls=%fused_computation.17 | convolution fusion | flops 5373952000 | bytes 9449472 | tf_op jit(solution)/shard_map/ept,td->epd/dot_general | solution.py:49
  159.1 2.4 copy-done.10
  161.5 4.0 fusion.34
  165.5 8.8 %fusion.6 = bf16[2,640,2048]{2,1,0:T(8,128)(2,1)S(1)} fusion(bf16[1024,4224]{0,1:T(8,128)(2,1)} %all-gather.2.cloned.1.call-done, s32[2,1024]{1,0:T(2,128)S(1)} %compare_select_fusion.1), kind=kOutput, calls=%fused_computation.16 | convolution fusion | flops 5373952000 | bytes 9445376 | tf_op jit(solution)/shard_map/ept,td->epd/dot_general | solution.py:46
  174.3 4.1 fusion.33
  178.4 6.1 %multiply_convert_fusion.2 = (bf16[2,640,384]{1,2,0:T(8,128)(2,1)S(1)}, bf16[2,640,384]{1,2,0:T(8,128)(2,1)S(1)}, bf16[2,640,384]{1,2,0:T(8,128)(2,1)}) fusion(f32[2,640,384]{1,2,0:T(8,128)} %fusion.33, f32[2,640,384]{1,2,0:T(8,128)} %fusion.34, bf16[2,640,2048]{2,1,0:T(8,128)(2,1)S(1)} %fusion.6, bf16[2,2048,384]{2,1,0:T(8,128)(2,1)S(1)} %copy-done), kind=kOutput, calls=%fused_computation.34 | convolution fusion | flops 2020638720 | bytes 15269888 | tf_op jit(solution)/shard_map/erd,edf->erf/dot_general | solution.py:9
  184.5 3.2 fusion.62
  187.7 7.3 %bitcast_convert_fusion.1 = bf16[1024,2048]{1,0:T(8,128)(2,1)} fusion(bf16[2,1024]{1,0:T(2,128)(2,1)S(1)} %fusion.28, s32[2,1024]{1,0:T(2,128)S(1)} %compare_select_fusion.1, bf16[2,640,2048]{2,1,0:T(8,128)(2,1)S(1)} %fusion.62), kind=kOutput, calls=%fused_computation.4 | convolution fusion | flops 5373427712 | bytes 9449472 | tf_op jit(solution)/shard_map/ept,epd->td/dot_general | solution.py:54
  195.1 5.8 %fusion.35 = f32[2,640,2048]{2,1,0:T(8,128)} fusion(bf16[2,640,384]{1,2,0:T(8,128)(2,1)S(1)} %get-tuple-element.28, bf16[2,2048,384]{2,1,0:T(8,128)(2,1)S(1)} %copy-done.2), kind=kOutput, calls=%fused_computation.63 | convolution fusion | flops 2013265920 | bytes 14614528 | tf_op jit(solution)/shard_map/erf,edf->erd/dot_general | solution.py:66
  200.9 15.0 %bitcast_convert_fusion = bf16[1024,2048]{1,0:T(8,128)(2,1)} fusion(f32[2,640,2048]{2,1,0:T(8,128)} %fusion.35, s32[2,1024]{1,0:T(2,128)S(1)} %compare_select_fusion.1, bf16[2,640,384]{1,2,0:T(8,128)(2,1)} %get-tuple-element.29, bf16[2,2048,384]{2,1,0:T(8,128)(2,1)S(1)} %copy-done), kind=kOutput, calls=%fused_computation.3 | convolution fusion | flops 7390625792 | bytes 18817024 | tf_op jit(solution)/shard_map/ept,epd->td/dot_general | solution.py:69
  215.9 7.9 %pad_maximum_fusion.1 = bf16[1024,4096]{1,0:T(8,128)(2,1)} fusion(bf16[1024,2048]{1,0:T(8,128)(2,1)} %bitcast_convert_fusion, bf16[1024,2048]{1,0:T(8,128)(2,1)} %bitcast_convert_fusion.1), kind=kLoop, calls=%fused_computation.2 | loop fusion | flops 16777216 | bytes 16777216 | tf_op jit(solution)/shard_map/concatenate | solution.py:73
  223.8 5.5 %fusion.10 = bf16[2048,2,384]{0,2,1:T(8,128)(2,1)S(1)} fusion(bf16[2,640,384]{1,2,0:T(8,128)(2,1)} %copy-done.8, bf16[2,640,2048]{2,1,0:T(8,128)(2,1)} %copy-done.10), kind=kOutput, calls=%fused_computation.19 | convolution fusion | flops 2014838784 | bytes 9371648 | tf_op jit(solution)/shard_map/erf,erd->def/dot_general | solution.py:81
  229.4 8.7 %convert_bitcast_fusion = bf16[2048,2,768]{0,2,1:T(8,128)(2,1)S(1)} fusion(bf16[2,640,2048]{2,1,0:T(8,128)(2,1)} %copy-done.9, bf16[2,640,384]{1,2,0:T(8,128)(2,1)S(1)} %copy-done.11, bf16[2,640,384]{1,2,0:T(8,128)(2,1)S(1)} %copy-done.4), kind=kOutput, calls=%fused_computation.5 | convolution fusion | flops 4033609728 | bytes 13500416 | tf_op jit(solution)/shard_map/erd,erf->def/dot_general | solution.py:78
  238.1 8.5 %pad_maximum_fusion = bf16[2048,2,1152]{0,2,1:T(8,128)(2,1)} fusion(bf16[2048,2,384]{0,2,1:T(8,128)(2,1)S(1)} %fusion.10, bf16[2048,2,768]{0,2,1:T(8,128)(2,1)S(1)} %convert_bitcast_fusion), kind=kLoop, calls=%fused_computation.1 | loop fusion | flops 18874368 | bytes 18874368 | tf_op jit(solution)/shard_map/concatenate | solution.py:83
  246.6 123.0 %reduce-scatter.3.cloned.1.call-done = bf16[128,4096]{1,0:T(8,128)(2,1)} async-done(((bf16[1024,4096]{1,0:T(8,128)(2,1)}), bf16[128,4096]{1,0:T(8,128)(2,1)}) %reduce-scatter.3.cloned.1.call-update) | async-done | bytes 1048592 | tf_op jit(solution)/shard_map/reduce_scatter | solution.py:72
  369.6 2.4 fusion.32
  372.0 77.1 %reduce-scatter.5.cloned.1.call-done = bf16[512,2,1152]{0,2,1:T(8,128)(2,1)} async-done(((bf16[2048,2,1152]{0,2,1:T(8,128)(2,1)}), bf16[512,2,1152]{0,2,1:T(8,128)(2,1)}) %reduce-scatter.5.cloned.1.call-update) | async-done | bytes 2359312 | tf_op jit(solution)/shard_map/reduce_scatter | solution.py:82
  449.1 3.1 slice_bitcast_fusion.8
  452.1 2.3 copy.53
  454.4 2.3 copy.52
  (44 shorter events, 5.9 us)
Async XLA Ops:
  7.2 171.2 %copy-start = (bf16[2,2048,384]{2,1,0:T(8,128)(2,1)S(1)}, bf16[2,2048,384]{2,1,0:T(8,128)(2,1)}, u32[]{:S(2)}) copy-start(bf16[2,2048,384]{2,1,0:T(8,128)(2,1)} %param.12) | copy-start | bytes 9437188
  7.2 8.1 %copy-start.5 = (s32[128,8]{0,1:T(8,128)S(1)}, s32[128,8]{0,1:T(8,128)}, u32[]{:S(2)}) copy-start(s32[128,8]{0,1:T(8,128)} %param.8) | copy-start | bytes 12292
  7.2 8.7 %copy-start.6 = (bf16[128,8]{0,1:T(8,128)(2,1)S(1)}, bf16[128,8]{0,1:T(8,128)(2,1)}, u32[]{:S(2)}) copy-start(bf16[128,8]{0,1:T(8,128)(2,1)} %param.9) | copy-start | bytes 6148
  7.2 140.9 %all-gather.2.cloned.1.call-start = ((), (), s32[]{:S(2)}) async-start(), calls=%async_computation.2 | async-start | bytes 9732096 | tf_op jit(solution)/shard_map/all_gather | solution.py:33
  17.1 352.5 %reduce-scatter.3.cloned.1.call-start = ((), (), s32[]{:S(2)}) async-start(), calls=%async_computation.3 | async-start | bytes 9437184 | tf_op jit(solution)/shard_map/reduce_scatter | solution.py:72
  150.2 11.3 %copy-start.7 = (bf16[2,384,2048]{2,1,0:T(8,128)(2,1)S(1)}, bf16[2,384,2048]{2,1,0:T(8,128)(2,1)}, u32[]{:S(2)}) copy-start(bf16[2,384,2048]{2,1,0:T(8,128)(2,1)} %param.13) | copy-start | bytes 9437188
  159.1 2.4 copy-start.10
  165.4 8.8 %copy-start.2 = (bf16[2,2048,384]{2,1,0:T(8,128)(2,1)S(1)}, bf16[2,2048,384]{2,1,0:T(8,128)(2,1)}, u32[]{:S(2)}) copy-start(bf16[2,2048,384]{2,1,0:T(8,128)(2,1)} %param.11) | copy-start | bytes 9437188
  174.3 4.1 copy-start.9
  184.5 3.2 copy-start.8
  184.5 10.6 %copy-start.3 = (bf16[2,640,384]{1,2,0:T(8,128)(2,1)}, bf16[2,640,384]{1,2,0:T(8,128)(2,1)S(1)}, u32[]{:S(2)}) copy-start(bf16[2,640,384]{1,2,0:T(8,128)(2,1)S(1)} %get-tuple-element.28) | copy-start | bytes 2949124
  223.8 225.3 %reduce-scatter.5.cloned.1.call-start = ((), (), s32[]{:S(2)}) async-start(), calls=%async_computation.4 | async-start | bytes 11796480 | tf_op jit(solution)/shard_map/reduce_scatter | solution.py:82
  223.8 5.6 %copy-start.4 = (bf16[2,640,384]{1,2,0:T(8,128)(2,1)S(1)}, bf16[2,640,384]{1,2,0:T(8,128)(2,1)}, u32[]{:S(2)}) copy-start(bf16[2,640,384]{1,2,0:T(8,128)(2,1)} %copy-done.3) | copy-start | bytes 2949124
  223.8 5.6 %copy-start.11 = (bf16[2,640,384]{1,2,0:T(8,128)(2,1)S(1)}, bf16[2,640,384]{1,2,0:T(8,128)(2,1)}, u32[]{:S(2)}) copy-start(bf16[2,640,384]{1,2,0:T(8,128)(2,1)} %get-tuple-element.29) | copy-start | bytes 2949124
  369.6 87.1 %copy-start.1 = (bf16[2,2048,384]{2,1,0:T(8,128)(2,1)S(1)}, bf16[2,2048,384]{2,1,0:T(8,128)(2,1)}, u32[]{:S(2)}) copy-start(bf16[2,2048,384]{2,1,0:T(8,128)(2,1)} %param.12) | copy-start | bytes 9437188
Sparse Core Ops, SparseCore 0:
  17.2 130.8 all-gather.1
  223.9 145.6 reduce-scatter.2
  372.2 76.8 reduce-scatter.4

commit v3 on v2

--- a/solution.py
+++ b/solution.py
@@ -69,11 +69,7 @@
     grad_part = jnp.einsum(
         "ept,epd->td", pick_x, row_grads, preferred_element_type=jnp.float32
     ).astype(jnp.bfloat16)
-    returned = lax.psum_scatter(
-        jnp.concatenate([out_part, grad_part], axis=1), "dp", scatter_dimension=0, tiled=True
-    )
-    layer_out = returned[:, :width]
-    grad_tokens = returned[:, width:]
+    grad_tokens = lax.psum_scatter(grad_part, "dp", scatter_dimension=0, tiled=True)
     both_factors = jnp.concatenate([grad_gateact, grad_upact], axis=2)
     input_term = jnp.einsum(
         "erd,erf->def", arrived, both_factors, preferred_element_type=jnp.float32

time: 464 us -> 462 us (level)
  waiting for transfers between devices: 331 us -> 346 us
  other arithmetic: 18.7 us -> 10.9 us
  local copies, waits for them, and re-layouts: 21.9 us -> 17.1 us
    reduce_scatter x1 -> x2, waiting for transfers between devices: 123 us -> 177 us  [the longest x1 92 us: body(): lax.psum_scatter(grad_part, 'dp', scatter_dimension=0, tiled=True)]
    reduce_scatter x1, waiting for transfers between devices: 77.1 us -> 37.9 us  [body(): lax.psum_scatter(jnp.concatenate([input_term, down_term], axis=2).astype(...]
    concatenate x1 -> x0, other arithmetic: 7.86 us -> none  [body(): jnp.concatenate([out_part, grad_part], axis=1)]
    unnamed x32 -> x24, local copies, waits for them, and re-layouts: 15.6 us -> 13.2 us
  transfers between devices with their start and end apart: 3 -> 4, of which waited for: 3 -> 4; matrix products, arithmetic and copies ran while one was open for 5% -> 10% of each run, Pallas kernels for 0% -> 0%
where the time goes in v3:
time: 462 us; the launch traced here: 461 us
  waiting for transfers between devices  346 us (75%)
  matrix products  72.9 us (16%)
  local copies, waits for them, and re-layouts  17.1 us (4%)
  between operations  14 us (3%)
  other arithmetic  10.9 us (2%)
    all_gather x1, waiting for transfers between devices, body(): all_both = lax.all_gather(both, 'dp', axis=0, tiled=True)  131 us
    reduce_scatter x1, waiting for transfers between devices, body(): lax.psum_scatter(grad_part, 'dp', scatter_dimension=0, tiled=True)  92 us
    reduce_scatter x1, waiting for transfers between devices, body(): lax.psum_scatter(out_part, 'dp', scatter_dimension=0, tiled=True)  84.9 us
    reduce_scatter x1, waiting for transfers between devices, body(): lax.psum_scatter(jnp.concatenate([input_term, down_term], axis=2).astype(...  37.9 us
    dot_general x1, matrix products, body(): jnp.einsum('ept,epd->td', pick_x, row_grads, preferred_element_type=jnp.f...  16.4 us
    unnamed x24, local copies, waits for them, and re-layouts  13.2 us
    dot_general x1, matrix products, body(): jnp.einsum('erf,edf->erd', grad_gateact, w_gate, preferred_element_type=j...  9.58 us
  transfers between devices with their start and end apart: 4, of which 4 were waited for; matrix products, arithmetic and copies ran while one was open for 10% of the time, Pallas kernels for 0%

profile of v3, /device:TPU:0, one launch (start us, length us, event | category | flops | bytes accessed | tf_op | source)
XLA Modules:
  0.0 461.0 jit_solution(14644032707693486490)
XLA Ops:
  7.2 2.2 copy.41
  9.4 2.0 copy.42
  11.5 1.9 constant_dynamic-update-slice_fusion.3
  13.4 1.9 constant_dynamic-update-slice_fusion.2
  17.1 130.9 %all-gather.2.cloned.1.call-done = bf16[1024,4224]{0,1:T(8,128)(2,1)} async-done(((bf16[128,4224]{0,1:T(8,128)(2,1)}), bf16[1024,4224]{0,1:T(8,128)(2,1)}) %all-gather.2.cloned.1.call-update) | async-done | bytes 8650768 | tf_op jit(solution)/shard_map/all_gather | solution.py:33
  148.1 0.7 slice_convert_fusion.1
  150.2 8.8 %fusion.6 = bf16[2,640,2048]{2,1,0:T(8,128)(2,1)S(1)} fusion(bf16[1024,4224]{0,1:T(8,128)(2,1)} %all-gather.2.cloned.1.call-done, s32[2,1024]{1,0:T(2,128)S(1)} %compare_select_fusion.1), kind=kOutput, calls=%fused_computation.15 | convolution fusion | flops 5373952000 | bytes 9445376 | tf_op jit(solution)/shard_map/ept,td->epd/dot_general | solution.py:46
  159.0 2.9 fusion.33
  161.9 2.9 fusion.32
  164.8 8.9 %fusion.7 = bf16[2,640,2048]{2,1,0:T(8,128)(2,1)S(1)} fusion(bf16[1024,4224]{0,1:T(8,128)(2,1)} %all-gather.2.cloned.1.call-done, bf16[2,1024]{1,0:T(2,128)(2,1)S(1)} %fusion.28, s32[2,1024]{1,0:T(2,128)S(1)} %compare_select_fusion.1), kind=kOutput, calls=%fused_computation.16 | convolution fusion | flops 5373952000 | bytes 9449472 | tf_op jit(solution)/shard_map/ept,td->epd/dot_general | solution.py:49
  173.7 3.4 multiply_convert_fusion
  177.2 2.8 fusion.10
  180.1 5.3 %convert_bitcast_fusion = bf16[2048,2,768]{0,2,1:T(8,128)(2,1)S(1)} fusion(bf16[2,640,2048]{2,1,0:T(8,128)(2,1)S(1)} %fusion.6, bf16[2,640,384]{1,2,0:T(8,128)(2,1)S(1)} %get-tuple-element.27, bf16[2,640,384]{1,2,0:T(8,128)(2,1)S(1)} %get-tuple-element.28), kind=kOutput, calls=%fused_computation.4 | convolution fusion | flops 4033609728 | bytes 13500416 | tf_op jit(solution)/shard_map/erd,erf->def/dot_general | solution.py:74
  185.4 8.4 %pad_maximum_fusion = bf16[2048,2,1152]{0,2,1:T(8,128)(2,1)} fusion(bf16[2048,2,384]{0,2,1:T(8,128)(2,1)S(1)} %fusion.10, bf16[2048,2,768]{0,2,1:T(8,128)(2,1)S(1)} %convert_bitcast_fusion), kind=kLoop, calls=%fused_computation.1 | loop fusion | flops 18874368 | bytes 18874368 | tf_op jit(solution)/shard_map/concatenate | solution.py:79
  193.9 4.4 fusion.61
  198.3 7.4 %bitcast_convert_fusion.1 = bf16[1024,2048]{1,0:T(8,128)(2,1)} fusion(bf16[2,1024]{1,0:T(2,128)(2,1)S(1)} %fusion.28, s32[2,1024]{1,0:T(2,128)S(1)} %compare_select_fusion.1, bf16[2,640,2048]{2,1,0:T(8,128)(2,1)S(1)} %fusion.61), kind=kOutput, calls=%fused_computation.3 | convolution fusion | flops 5373427712 | bytes 9449472 | tf_op jit(solution)/shard_map/ept,epd->td/dot_general | solution.py:54
  206.0 9.6 %fusion.34 = f32[2,640,2048]{2,1,0:T(8,128)} fusion(bf16[2,640,384]{1,2,0:T(8,128)(2,1)} %copy-done.2, bf16[2,2048,384]{2,1,0:T(8,128)(2,1)} %param.11), kind=kOutput, calls=%fused_computation.61 | convolution fusion | flops 2013265920 | bytes 14614528 | tf_op jit(solution)/shard_map/erf,edf->erd/dot_general | solution.py:66
  215.6 16.4 %bitcast_convert_fusion = bf16[1024,2048]{1,0:T(8,128)(2,1)} fusion(f32[2,640,2048]{2,1,0:T(8,128)} %fusion.34, s32[2,1024]{1,0:T(2,128)S(1)} %compare_select_fusion.1, bf16[2,640,384]{1,2,0:T(8,128)(2,1)} %copy-done.7, bf16[2,2048,384]{2,1,0:T(8,128)(2,1)} %param.12), kind=kOutput, calls=%fused_computation.2 | convolution fusion | flops 7390625792 | bytes 18817024 | tf_op jit(solution)/shard_map/ept,epd->td/dot_general | solution.py:69
  232.0 37.9 %reduce-scatter.8.cloned.1.call-done = bf16[512,2,1152]{0,2,1:T(8,128)(2,1)} async-done(((bf16[2048,2,1152]{0,2,1:T(8,128)(2,1)}), bf16[512,2,1152]{0,2,1:T(8,128)(2,1)}) %reduce-scatter.8.cloned.1.call-update) | async-done | bytes 2359312 | tf_op jit(solution)/shard_map/reduce_scatter | solution.py:78
  269.9 3.1 slice_bitcast_fusion.8
  273.0 2.3 copy.53
  275.3 2.3 copy.52
  277.5 84.9 %reduce-scatter.4.cloned.1.call-done = bf16[128,2048]{1,0:T(8,128)(2,1)} async-done(((bf16[1024,2048]{1,0:T(8,128)(2,1)}), bf16[128,2048]{1,0:T(8,128)(2,1)}) %reduce-scatter.4.cloned.1.call-update) | async-done | bytes 524304 | tf_op jit(solution)/shard_map/reduce_scatter | solution.py:57
  362.4 92.0 %reduce-scatter.6.cloned.1.call-done = bf16[128,2048]{1,0:T(8,128)(2,1)} async-done(((bf16[1024,2048]{1,0:T(8,128)(2,1)}), bf16[128,2048]{1,0:T(8,128)(2,1)}) %reduce-scatter.6.cloned.1.call-update) | async-done | bytes 524304 | tf_op jit(solution)/shard_map/reduce_scatter | solution.py:72
  (37 shorter events, 3.5 us)
Async XLA Ops:
  7.2 166.6 %copy-start = (bf16[2,384,2048]{2,1,0:T(8,128)(2,1)S(1)}, bf16[2,384,2048]{2,1,0:T(8,128)(2,1)}, u32[]{:S(2)}) copy-start(bf16[2,384,2048]{2,1,0:T(8,128)(2,1)} %param.13) | copy-start | bytes 9437188
  7.2 8.1 %copy-start.3 = (s32[128,8]{0,1:T(8,128)S(1)}, s32[128,8]{0,1:T(8,128)}, u32[]{:S(2)}) copy-start(s32[128,8]{0,1:T(8,128)} %param.8) | copy-start | bytes 12292
  7.2 8.7 %copy-start.4 = (bf16[128,8]{0,1:T(8,128)(2,1)S(1)}, bf16[128,8]{0,1:T(8,128)(2,1)}, u32[]{:S(2)}) copy-start(bf16[128,8]{0,1:T(8,128)(2,1)} %param.9) | copy-start | bytes 6148
  7.2 140.9 %all-gather.2.cloned.1.call-start = ((), (), s32[]{:S(2)}) async-start(), calls=%async_computation.3 | async-start | bytes 9732096 | tf_op jit(solution)/shard_map/all_gather | solution.py:33
  17.1 252.8 %reduce-scatter.8.cloned.1.call-start = ((), (), s32[]{:S(2)}) async-start(), calls=%async_computation.6 | async-start | bytes 11796480 | tf_op jit(solution)/shard_map/reduce_scatter | solution.py:78
  150.1 8.9 %copy-start.5 = (bf16[2,2048,384]{2,1,0:T(8,128)(2,1)S(1)}, bf16[2,2048,384]{2,1,0:T(8,128)(2,1)}, u32[]{:S(2)}) copy-start(bf16[2,2048,384]{2,1,0:T(8,128)(2,1)} %param.12) | copy-start | bytes 9437188
  159.0 2.9 copy-start.1
  177.2 2.9 copy-start.6
  177.2 2.9 copy-start.2
  177.2 2.9 copy-start.7
  193.8 168.6 %reduce-scatter.4.cloned.1.call-start = ((), (), s32[]{:S(2)}) async-start(), calls=%async_computation.4 | async-start | bytes 4718592 | tf_op jit(solution)/shard_map/reduce_scatter | solution.py:57
  205.7 248.8 %reduce-scatter.6.cloned.1.call-start = ((), (), s32[]{:S(2)}) async-start(), calls=%async_computation.5 | async-start | bytes 4718592 | tf_op jit(solution)/shard_map/reduce_scatter | solution.py:72
Sparse Core Ops, SparseCore 0:
  17.2 130.8 all-gather.1
  194.0 75.9 reduce-scatter.7
  274.1 88.2 reduce-scatter.3
  366.5 87.9 reduce-scatter.5
